TPU v7x, 1024 devices: a whole 4x4x32 slice. The times are simulated.
1024 devices in a mesh: section: 4 (over z_hi), expert: 32 (over z_lo, x), hidden: 8 (over y, core).
Axes of the slice: x: 4, y: 4, z: 32 (z_hi: 4, z_lo: 8; z = z_hi * 8 + z_lo), core: 2. Of those that a mesh axis runs over, the one named last changes fastest.
Arguments:
- tokens: bfloat16 [4, 512, 7168], P(None, 'expert', 'hidden'), may hold values from -12 to 12
- gate_up: bfloat16 [4, 7168, 2, 16384], P('section', 'hidden', None, 'expert'), may hold values from -0.0625 to 0.0625
- down_proj: bfloat16 [4, 16384, 7168], P('section', 'expert', 'hidden'), may hold values from -0.1875 to 0.1875
- routes: int32 [4, 4, 512, 2], P('section', None, 'expert'), may hold values from 0 to 15, all different within a row; in each aligned block of 16 rows (0 to 15, 16 to 31, ..., all dimensions but the last counted through in order) at most 3 rows name the same one
- gate_weights: bfloat16 [4, 4, 512, 2], P('section', None, 'expert'), may hold values from 0.099609375 to 0.59765625
Outputs:
- layer_outputs: bfloat16 [4, 4, 512, 7168], P('section', None, 'expert', 'hidden')
Inputs may be any that keep to these rules, and one draw needn't show every extreme that they name: `routes`: in every layer and micro-batch a token names 2 different experts, and the 16 tokens of one device (aligned blocks of 16 rows) name any one expert at most 3 times; some expert is named exactly 3 times in some block.
All inputs are finite; a program needn't handle non-finite values.
Results may differ from a plain program's by a relative error of at most 0.008.
Values may be sent and summed in bfloat16 or wider, within the bound.
A program may use at most 32 MiB of HBM per device.

v0:
```python
import math

import jax
import jax.numpy as jnp
from jax import lax
from jax.sharding import PartitionSpec as P

D = 7168
FFE = 1024
CAP = 3


EPS = 1e-06


def split_up(shard, dim, devices):
    before, after = (shard.shape[:dim], shard.shape[dim + 1 :])
    return jnp.moveaxis(shard.reshape(*before, devices, -1, *after), dim, 0)


def sum_at_owner(shard, axis, dim):
    parts = split_up(shard, dim, lax.axis_size(axis))
    arrived = lax.all_to_all(parts, axis, split_axis=0, concat_axis=0, tiled=True)
    return arrived.sum(axis=0)


def side_by_side(arrays, axis, dim, along):
    widths = [math.prod(a.shape[along:]) for a in arrays]
    both = jnp.concatenate(
        [a.reshape(*a.shape[:along], w) for a, w in zip(arrays, widths)], axis=along
    )
    out = sum_at_owner(both, axis, dim)
    parts = jnp.split(out, [sum(widths[:k]) for k in range(1, len(widths))], axis=along)
    return tuple((b.reshape(*out.shape[:along], *a.shape[along:]) for a, b in zip(arrays, parts)))


def copy_for_each(shard, axis):
    copies = jnp.broadcast_to(shard, (lax.axis_size(axis), *shard.shape))
    return lax.all_to_all(copies, axis, split_axis=0, concat_axis=0, tiled=True)


def laid_out(parts, dim):
    parts = jnp.moveaxis(parts, 0, dim)
    shape = parts.shape
    return parts.reshape(*shape[:dim], shape[dim] * shape[dim + 1], *shape[dim + 2 :])


def collect(shard, axis, dim):
    parts = copy_for_each(shard, axis)
    return laid_out(parts, dim)


def shifted(value, axis, steps):
    count = lax.axis_size(axis)
    first, last = (max(0, -steps), min(count, count - steps))
    return lax.ppermute(value, axis, [(source, source + steps) for source in range(first, last)])


def on_device(tokens, gate_up, down_proj, routes, gate_weights):
    sections = lax.axis_size("section")
    peers = lax.axis_size("expert")
    section_id = lax.axis_index("section")
    micro_count, tok_rows, slice_width = tokens.shape
    units_dev = gate_up.shape[3]
    local_units = min(FFE, units_dev)
    local_count = units_dev // local_units
    slot_rows_count = peers * CAP
    slot_count = peers * local_count
    device_ids = jnp.arange(peers, dtype=jnp.int32)
    local_ids = jnp.arange(local_count, dtype=jnp.int32)
    slot_expert = (device_ids[:, None] * units_dev // FFE + local_ids[None, :]).reshape(slot_count)
    capacity_ids = jnp.arange(CAP, dtype=jnp.int32)
    w_in = gate_up[0].reshape(slice_width, 2, local_count, local_units)
    w_in = w_in.transpose(2, 0, 1, 3)
    w_in = w_in.reshape(local_count, slice_width, 2 * local_units)
    w_out = down_proj[0].reshape(local_count, local_units, slice_width)

    def source_tables(route_rows, gate_rows):
        matches = route_rows[:, :, None] == slot_expert[None, None, :]
        chosen = jnp.sum(matches.astype(jnp.int32), axis=1, dtype=jnp.int32)
        weight_dense = jnp.sum(
            jnp.where(matches, gate_rows.astype(jnp.float32)[:, :, None], jnp.float32(0.0)), axis=1
        )
        rank = jnp.cumsum(chosen, axis=0, dtype=jnp.int32) - chosen
        hits = (rank[None, :, :] == capacity_ids[:, None, None]) & (chosen[None, :, :] == 1)
        hits = (
            jnp.transpose(hits, (2, 0, 1)).reshape(slot_count * CAP, tok_rows).astype(jnp.float32)
        )
        spread_weight = jnp.repeat(weight_dense.T, CAP, axis=0)
        return (hits.astype(jnp.bfloat16), (hits * spread_weight).astype(jnp.bfloat16))

    def expert_outputs(expert_rows):
        projected = jnp.einsum(
            "jrd,jdf->jrf", expert_rows, w_in, preferred_element_type=jnp.float32
        )
        widened = expert_rows.astype(jnp.float32)
        squares = jnp.sum(widened * widened, axis=2)
        summed, summed_squares = side_by_side((projected, squares), "hidden", 1, 2)
        norm_scale = lax.rsqrt(summed_squares / D + EPS)[:, :, None]
        activated = (
            jax.nn.silu(norm_scale * summed[:, :, :local_units])
            * (norm_scale * summed[:, :, local_units:])
        ).astype(jnp.bfloat16)
        return jnp.einsum(
            "jrf,jfd->jrd",
            collect(activated, "hidden", 1),
            w_out,
            preferred_element_type=jnp.float32,
        ).astype(jnp.bfloat16)

    def run_layer(current, safe_index):
        route_rows = lax.dynamic_index_in_dim(routes[0], safe_index, 0, keepdims=False)
        gate_rows = lax.dynamic_index_in_dim(gate_weights[0], safe_index, 0, keepdims=False)
        placement, combiner = source_tables(route_rows, gate_rows)
        sent = jnp.dot(placement, current, preferred_element_type=jnp.float32).astype(jnp.bfloat16)
        received = lax.all_to_all(sent, "expert", split_axis=0, concat_axis=0, tiled=True)
        expert_rows = (
            received.reshape(peers, local_count, CAP, slice_width)
            .transpose(1, 0, 2, 3)
            .reshape(local_count, slot_rows_count, slice_width)
        )
        out_rows = expert_outputs(expert_rows)
        outgoing = (
            out_rows.reshape(local_count, peers, CAP, slice_width)
            .transpose(1, 0, 2, 3)
            .reshape(slot_count * CAP, slice_width)
        )
        returned = lax.all_to_all(outgoing, "expert", split_axis=0, concat_axis=0, tiled=True)
        mixed = lax.dot_general(
            combiner, returned, (((0,), (0,)), ((), ())), preferred_element_type=jnp.float32
        )
        return (current.astype(jnp.float32) + mixed).astype(jnp.bfloat16)

    def tick(step, carried):
        previous, saved = carried
        incoming = shifted(previous, "section", 1)
        batch_index = step - section_id
        valid = (batch_index >= 0) & (batch_index < micro_count)
        safe_index = jnp.clip(batch_index, 0, micro_count - 1)
        fresh = lax.dynamic_index_in_dim(tokens, safe_index, 0, keepdims=False)
        current = jnp.where(section_id == 0, fresh, incoming)
        computed = run_layer(current, safe_index)
        result = jnp.where(valid, computed, current)
        updated = lax.dynamic_update_index_in_dim(saved, result[None], safe_index, 0)
        saved = jnp.where(valid, updated, saved)
        return (result, saved)

    ticks = sections + micro_count - 1
    start_state = jnp.zeros((tok_rows, slice_width), jnp.bfloat16)
    start_saved = jnp.zeros((micro_count, tok_rows, slice_width), jnp.bfloat16)
    _, saved = lax.fori_loop(0, ticks, tick, (start_state, start_saved))
    return saved[None]


def solution(mesh):
    placed = (
        P(None, "expert", "hidden"),
        P("section", "hidden", None, "expert"),
        P("section", "expert", "hidden"),
        P("section", None, "expert", None),
        P("section", None, "expert", None),
    )
    return jax.shard_map(
        on_device,
        mesh=mesh,
        in_specs=placed,
        out_specs=P("section", None, "expert", "hidden"),
        check_vma=False,
    )
```

profile of v0, /device:TPU:8, one launch (start us, length us, event | category | flops | bytes accessed | tf_op | source)
XLA Modules:
  0.0 627.8 jit_solution(5053693361413637674)
XLA Ops:
  5.3 622.5 %while.18 = (s32[]{:T(128)}, bf16[16,896]{1,0:T(8,128)(2,1)S(1)}, bf16[4,16,896]{2,1,0:T(8,128)(2,1)}, s32[]{:T(128)}, pred[]{:T(512)}, /*index=5*/bf16[4,16,896...) while((s32[]{:T(128)}, bf16[16,896]{1,0:T(8,128)(2,1)S(1)}, ...), condition=%wide.region_6.7_spmd.clone.clone, body=%wide.region_0.6_spmd.clone.clone.sunk | while | flops 270549632 | bytes 9971757 | solution.py:151
  5.3 15.7 %collective-permute-start = (bf16[16,896]{1,0:T(8,128)(2,1)S(1)}, bf16[16,896]{1,0:T(8,128)(2,1)S(1)}, u32[]{:S(2)}, u32[]{:S(2)}) collective-permute-start(bf16[16,896]{1,0:T(8,128)(2,1)S(1)} %broadcast_select_fusion.2), channel_id=1, source_target_pairs={{0,256},{256,512},{512,768},{1,257},{257,513},{513,769},{2,258},{2... | collective-permute-start | bytes 86024 | tf_op jit(solution)/shard_map/while/body/eval_jaxpr/ppermute | solution.py:56
  22.9 33.6 %all_to_all.66 = bf16[32,3,896]{2,1,0:T(4,128)(2,1)S(1)} all-to-all(bf16[32,3,896]{2,1,0:T(4,128)(2,1)S(1)} %all_to_all.56), channel_id=1, replica_groups=mesh['section'=4,'expert'=32,'hidden'=8] {'expert'}, dimensions={0} | all-to-all | bytes 344064 | tf_op jit(solution)/shard_map/while/body/eval_jaxpr/all_to_all | solution.py:116
  58.0 12.7 %all_to_all.67 = f32[8,1,12,1025]{3,1,2,0:T(1,128)S(1)} all-to-all(f32[8,1,12,1025]{3,1,2,0:T(1,128)S(1)} %copy.67), channel_id=1, replica_groups=mesh['section'=4,'expert'=32,'hidden'=8] {'hidden'}, dimensions={0} | all-to-all | bytes 787200 | tf_op jit(solution)/shard_map/while/body/eval_jaxpr/all_to_all | solution.py:23
  71.3 8.5 %all_to_all.68 = bf16[8,1,12,512]{3,2,1,0:T(8,128)(2,1)S(1)} all-to-all(bf16[8,1,12,512]{3,2,1,0:T(8,128)(2,1)S(1)} %broadcast_in_dim.109), channel_id=1, replica_groups=mesh['section'=4,'expert'=32,'hidden'=8] {'hidden'}, dimensions={0} | all-to-all | bytes 196608 | tf_op jit(solution)/shard_map/while/body/eval_jaxpr/all_to_all | solution.py:39
  87.0 17.1 %all-to-all-done.3 = bf16[32,3,896]{2,1,0:T(4,128)(2,1)S(1)} async-done(((bf16[32,3,896]{2,1,0:T(4,128)(2,1)}), bf16[32,3,896]{2,1,0:T(4,128)(2,1)S(1)}, u32[]{:S(2)}, u32[]{:S(2)}) %all-to-all-start.3) | async-done | bytes 172064 | tf_op jit(solution)/shard_map/while/body/eval_jaxpr/all_to_all | solution.py:128
  105.6 13.2 %collective-permute-start = (bf16[16,896]{1,0:T(8,128)(2,1)S(1)}, bf16[16,896]{1,0:T(8,128)(2,1)S(1)}, u32[]{:S(2)}, u32[]{:S(2)}) collective-permute-start(bf16[16,896]{1,0:T(8,128)(2,1)S(1)} %broadcast_select_fusion.2), channel_id=1, source_target_pairs={{0,256},{256,512},{512,768},{1,257},{257,513},{513,769},{2,258},{2... | collective-permute-start | bytes 86024 | tf_op jit(solution)/shard_map/while/body/eval_jaxpr/ppermute | solution.py:56
  120.8 22.5 %all_to_all.66 = bf16[32,3,896]{2,1,0:T(4,128)(2,1)S(1)} all-to-all(bf16[32,3,896]{2,1,0:T(4,128)(2,1)S(1)} %all_to_all.56), channel_id=1, replica_groups=mesh['section'=4,'expert'=32,'hidden'=8] {'expert'}, dimensions={0} | all-to-all | bytes 344064 | tf_op jit(solution)/shard_map/while/body/eval_jaxpr/all_to_all | solution.py:116
  144.7 11.8 %all_to_all.67 = f32[8,1,12,1025]{3,1,2,0:T(1,128)S(1)} all-to-all(f32[8,1,12,1025]{3,1,2,0:T(1,128)S(1)} %copy.67), channel_id=1, replica_groups=mesh['section'=4,'expert'=32,'hidden'=8] {'hidden'}, dimensions={0} | all-to-all | bytes 787200 | tf_op jit(solution)/shard_map/while/body/eval_jaxpr/all_to_all | solution.py:23
  172.8 17.1 %all-to-all-done.3 = bf16[32,3,896]{2,1,0:T(4,128)(2,1)S(1)} async-done(((bf16[32,3,896]{2,1,0:T(4,128)(2,1)}), bf16[32,3,896]{2,1,0:T(4,128)(2,1)S(1)}, u32[]{:S(2)}, u32[]{:S(2)}) %all-to-all-start.3) | async-done | bytes 172064 | tf_op jit(solution)/shard_map/while/body/eval_jaxpr/all_to_all | solution.py:128
  191.5 14.7 %collective-permute-start = (bf16[16,896]{1,0:T(8,128)(2,1)S(1)}, bf16[16,896]{1,0:T(8,128)(2,1)S(1)}, u32[]{:S(2)}, u32[]{:S(2)}) collective-permute-start(bf16[16,896]{1,0:T(8,128)(2,1)S(1)} %broadcast_select_fusion.2), channel_id=1, source_target_pairs={{0,256},{256,512},{512,768},{1,257},{257,513},{513,769},{2,258},{2... | collective-permute-start | bytes 86024 | tf_op jit(solution)/shard_map/while/body/eval_jaxpr/ppermute | solution.py:56
  208.1 22.5 %all_to_all.66 = bf16[32,3,896]{2,1,0:T(4,128)(2,1)S(1)} all-to-all(bf16[32,3,896]{2,1,0:T(4,128)(2,1)S(1)} %all_to_all.56), channel_id=1, replica_groups=mesh['section'=4,'expert'=32,'hidden'=8] {'expert'}, dimensions={0} | all-to-all | bytes 344064 | tf_op jit(solution)/shard_map/while/body/eval_jaxpr/all_to_all | solution.py:116
  232.0 11.8 %all_to_all.67 = f32[8,1,12,1025]{3,1,2,0:T(1,128)S(1)} all-to-all(f32[8,1,12,1025]{3,1,2,0:T(1,128)S(1)} %copy.67), channel_id=1, replica_groups=mesh['section'=4,'expert'=32,'hidden'=8] {'hidden'}, dimensions={0} | all-to-all | bytes 787200 | tf_op jit(solution)/shard_map/while/body/eval_jaxpr/all_to_all | solution.py:23
  260.1 17.1 %all-to-all-done.3 = bf16[32,3,896]{2,1,0:T(4,128)(2,1)S(1)} async-done(((bf16[32,3,896]{2,1,0:T(4,128)(2,1)}), bf16[32,3,896]{2,1,0:T(4,128)(2,1)S(1)}, u32[]{:S(2)}, u32[]{:S(2)}) %all-to-all-start.3) | async-done | bytes 172064 | tf_op jit(solution)/shard_map/while/body/eval_jaxpr/all_to_all | solution.py:128
  278.8 14.7 %collective-permute-start = (bf16[16,896]{1,0:T(8,128)(2,1)S(1)}, bf16[16,896]{1,0:T(8,128)(2,1)S(1)}, u32[]{:S(2)}, u32[]{:S(2)}) collective-permute-start(bf16[16,896]{1,0:T(8,128)(2,1)S(1)} %broadcast_select_fusion.2), channel_id=1, source_target_pairs={{0,256},{256,512},{512,768},{1,257},{257,513},{513,769},{2,258},{2... | collective-permute-start | bytes 86024 | tf_op jit(solution)/shard_map/while/body/eval_jaxpr/ppermute | solution.py:56
  295.3 22.5 %all_to_all.66 = bf16[32,3,896]{2,1,0:T(4,128)(2,1)S(1)} all-to-all(bf16[32,3,896]{2,1,0:T(4,128)(2,1)S(1)} %all_to_all.56), channel_id=1, replica_groups=mesh['section'=4,'expert'=32,'hidden'=8] {'expert'}, dimensions={0} | all-to-all | bytes 344064 | tf_op jit(solution)/shard_map/while/body/eval_jaxpr/all_to_all | solution.py:116
  319.2 11.8 %all_to_all.67 = f32[8,1,12,1025]{3,1,2,0:T(1,128)S(1)} all-to-all(f32[8,1,12,1025]{3,1,2,0:T(1,128)S(1)} %copy.67), channel_id=1, replica_groups=mesh['section'=4,'expert'=32,'hidden'=8] {'hidden'}, dimensions={0} | all-to-all | bytes 787200 | tf_op jit(solution)/shard_map/while/body/eval_jaxpr/all_to_all | solution.py:23
  331.7 8.5 %all_to_all.68 = bf16[8,1,12,512]{3,2,1,0:T(8,128)(2,1)S(1)} all-to-all(bf16[8,1,12,512]{3,2,1,0:T(8,128)(2,1)S(1)} %broadcast_in_dim.109), channel_id=1, replica_groups=mesh['section'=4,'expert'=32,'hidden'=8] {'hidden'}, dimensions={0} | all-to-all | bytes 196608 | tf_op jit(solution)/shard_map/while/body/eval_jaxpr/all_to_all | solution.py:39
  347.4 17.1 %all-to-all-done.3 = bf16[32,3,896]{2,1,0:T(4,128)(2,1)S(1)} async-done(((bf16[32,3,896]{2,1,0:T(4,128)(2,1)}), bf16[32,3,896]{2,1,0:T(4,128)(2,1)S(1)}, u32[]{:S(2)}, u32[]{:S(2)}) %all-to-all-start.3) | async-done | bytes 172064 | tf_op jit(solution)/shard_map/while/body/eval_jaxpr/all_to_all | solution.py:128
  366.0 14.7 %collective-permute-start = (bf16[16,896]{1,0:T(8,128)(2,1)S(1)}, bf16[16,896]{1,0:T(8,128)(2,1)S(1)}, u32[]{:S(2)}, u32[]{:S(2)}) collective-permute-start(bf16[16,896]{1,0:T(8,128)(2,1)S(1)} %broadcast_select_fusion.2), channel_id=1, source_target_pairs={{0,256},{256,512},{512,768},{1,257},{257,513},{513,769},{2,258},{2... | collective-permute-start | bytes 86024 | tf_op jit(solution)/shard_map/while/body/eval_jaxpr/ppermute | solution.py:56
  382.6 22.5 %all_to_all.66 = bf16[32,3,896]{2,1,0:T(4,128)(2,1)S(1)} all-to-all(bf16[32,3,896]{2,1,0:T(4,128)(2,1)S(1)} %all_to_all.56), channel_id=1, replica_groups=mesh['section'=4,'expert'=32,'hidden'=8] {'expert'}, dimensions={0} | all-to-all | bytes 344064 | tf_op jit(solution)/shard_map/while/body/eval_jaxpr/all_to_all | solution.py:116
  406.5 11.8 %all_to_all.67 = f32[8,1,12,1025]{3,1,2,0:T(1,128)S(1)} all-to-all(f32[8,1,12,1025]{3,1,2,0:T(1,128)S(1)} %copy.67), channel_id=1, replica_groups=mesh['section'=4,'expert'=32,'hidden'=8] {'hidden'}, dimensions={0} | all-to-all | bytes 787200 | tf_op jit(solution)/shard_map/while/body/eval_jaxpr/all_to_all | solution.py:23
  418.9 8.5 %all_to_all.68 = bf16[8,1,12,512]{3,2,1,0:T(8,128)(2,1)S(1)} all-to-all(bf16[8,1,12,512]{3,2,1,0:T(8,128)(2,1)S(1)} %broadcast_in_dim.109), channel_id=1, replica_groups=mesh['section'=4,'expert'=32,'hidden'=8] {'hidden'}, dimensions={0} | all-to-all | bytes 196608 | tf_op jit(solution)/shard_map/while/body/eval_jaxpr/all_to_all | solution.py:39
  434.6 17.1 %all-to-all-done.3 = bf16[32,3,896]{2,1,0:T(4,128)(2,1)S(1)} async-done(((bf16[32,3,896]{2,1,0:T(4,128)(2,1)}), bf16[32,3,896]{2,1,0:T(4,128)(2,1)S(1)}, u32[]{:S(2)}, u32[]{:S(2)}) %all-to-all-start.3) | async-done | bytes 172064 | tf_op jit(solution)/shard_map/while/body/eval_jaxpr/all_to_all | solution.py:128
  453.3 14.7 %collective-permute-start = (bf16[16,896]{1,0:T(8,128)(2,1)S(1)}, bf16[16,896]{1,0:T(8,128)(2,1)S(1)}, u32[]{:S(2)}, u32[]{:S(2)}) collective-permute-start(bf16[16,896]{1,0:T(8,128)(2,1)S(1)} %broadcast_select_fusion.2), channel_id=1, source_target_pairs={{0,256},{256,512},{512,768},{1,257},{257,513},{513,769},{2,258},{2... | collective-permute-start | bytes 86024 | tf_op jit(solution)/shard_map/while/body/eval_jaxpr/ppermute | solution.py:56
  469.8 22.5 %all_to_all.66 = bf16[32,3,896]{2,1,0:T(4,128)(2,1)S(1)} all-to-all(bf16[32,3,896]{2,1,0:T(4,128)(2,1)S(1)} %all_to_all.56), channel_id=1, replica_groups=mesh['section'=4,'expert'=32,'hidden'=8] {'expert'}, dimensions={0} | all-to-all | bytes 344064 | tf_op jit(solution)/shard_map/while/body/eval_jaxpr/all_to_all | solution.py:116
  493.8 11.8 %all_to_all.67 = f32[8,1,12,1025]{3,1,2,0:T(1,128)S(1)} all-to-all(f32[8,1,12,1025]{3,1,2,0:T(1,128)S(1)} %copy.67), channel_id=1, replica_groups=mesh['section'=4,'expert'=32,'hidden'=8] {'hidden'}, dimensions={0} | all-to-all | bytes 787200 | tf_op jit(solution)/shard_map/while/body/eval_jaxpr/all_to_all | solution.py:23
  521.9 17.1 %all-to-all-done.3 = bf16[32,3,896]{2,1,0:T(4,128)(2,1)S(1)} async-done(((bf16[32,3,896]{2,1,0:T(4,128)(2,1)}), bf16[32,3,896]{2,1,0:T(4,128)(2,1)S(1)}, u32[]{:S(2)}, u32[]{:S(2)}) %all-to-all-start.3) | async-done | bytes 172064 | tf_op jit(solution)/shard_map/while/body/eval_jaxpr/all_to_all | solution.py:128
  540.5 14.7 %collective-permute-start = (bf16[16,896]{1,0:T(8,128)(2,1)S(1)}, bf16[16,896]{1,0:T(8,128)(2,1)S(1)}, u32[]{:S(2)}, u32[]{:S(2)}) collective-permute-start(bf16[16,896]{1,0:T(8,128)(2,1)S(1)} %broadcast_select_fusion.2), channel_id=1, source_target_pairs={{0,256},{256,512},{512,768},{1,257},{257,513},{513,769},{2,258},{2... | collective-permute-start | bytes 86024 | tf_op jit(solution)/shard_map/while/body/eval_jaxpr/ppermute | solution.py:56
  557.1 22.5 %all_to_all.66 = bf16[32,3,896]{2,1,0:T(4,128)(2,1)S(1)} all-to-all(bf16[32,3,896]{2,1,0:T(4,128)(2,1)S(1)} %all_to_all.56), channel_id=1, replica_groups=mesh['section'=4,'expert'=32,'hidden'=8] {'expert'}, dimensions={0} | all-to-all | bytes 344064 | tf_op jit(solution)/shard_map/while/body/eval_jaxpr/all_to_all | solution.py:116
  581.0 11.8 %all_to_all.67 = f32[8,1,12,1025]{3,1,2,0:T(1,128)S(1)} all-to-all(f32[8,1,12,1025]{3,1,2,0:T(1,128)S(1)} %copy.67), channel_id=1, replica_groups=mesh['section'=4,'expert'=32,'hidden'=8] {'hidden'}, dimensions={0} | all-to-all | bytes 787200 | tf_op jit(solution)/shard_map/while/body/eval_jaxpr/all_to_all | solution.py:23
  609.1 17.1 %all-to-all-done.3 = bf16[32,3,896]{2,1,0:T(4,128)(2,1)S(1)} async-done(((bf16[32,3,896]{2,1,0:T(4,128)(2,1)}), bf16[32,3,896]{2,1,0:T(4,128)(2,1)S(1)}, u32[]{:S(2)}, u32[]{:S(2)}) %all-to-all-start.3) | async-done | bytes 172064 | tf_op jit(solution)/shard_map/while/body/eval_jaxpr/all_to_all | solution.py:128
  (256 shorter events, 127.1 us)
Async XLA Ops:
  0.0 5.3 copy-start
  0.0 5.3 copy-start.1
  5.3 17.3 %collective-permute-start = (bf16[16,896]{1,0:T(8,128)(2,1)S(1)}, bf16[16,896]{1,0:T(8,128)(2,1)S(1)}, u32[]{:S(2)}, u32[]{:S(2)}) collective-permute-start(bf16[16,896]{1,0:T(8,128)(2,1)S(1)} %broadcast_select_fusion.2), channel_id=1, source_target_pairs={{0,256},{256,512},{512,768},{1,257},{257,513},{513,769},{2,258},{2... | collective-permute-start | bytes 86024 | tf_op jit(solution)/shard_map/while/body/eval_jaxpr/ppermute | solution.py:56
  80.9 23.2 %all-to-all-start.3 = ((bf16[32,3,896]{2,1,0:T(4,128)(2,1)}), bf16[32,3,896]{2,1,0:T(4,128)(2,1)S(1)}, u32[]{:S(2)}, u32[]{:S(2)}) async-start(bf16[32,3,896]{2,1,0:T(4,128)(2,1)} %all_to_all.60), calls=%async_computation.3 | async-start | bytes 458752 | tf_op jit(solution)/shard_map/while/body/eval_jaxpr/all_to_all | solution.py:128
  105.6 14.8 %collective-permute-start = (bf16[16,896]{1,0:T(8,128)(2,1)S(1)}, bf16[16,896]{1,0:T(8,128)(2,1)S(1)}, u32[]{:S(2)}, u32[]{:S(2)}) collective-permute-start(bf16[16,896]{1,0:T(8,128)(2,1)S(1)} %broadcast_select_fusion.2), channel_id=1, source_target_pairs={{0,256},{256,512},{512,768},{1,257},{257,513},{513,769},{2,258},{2... | collective-permute-start | bytes 86024 | tf_op jit(solution)/shard_map/while/body/eval_jaxpr/ppermute | solution.py:56
  166.7 23.2 %all-to-all-start.3 = ((bf16[32,3,896]{2,1,0:T(4,128)(2,1)}), bf16[32,3,896]{2,1,0:T(4,128)(2,1)S(1)}, u32[]{:S(2)}, u32[]{:S(2)}) async-start(bf16[32,3,896]{2,1,0:T(4,128)(2,1)} %all_to_all.60), calls=%async_computation.3 | async-start | bytes 458752 | tf_op jit(solution)/shard_map/while/body/eval_jaxpr/all_to_all | solution.py:128
  191.5 16.3 %collective-permute-start = (bf16[16,896]{1,0:T(8,128)(2,1)S(1)}, bf16[16,896]{1,0:T(8,128)(2,1)S(1)}, u32[]{:S(2)}, u32[]{:S(2)}) collective-permute-start(bf16[16,896]{1,0:T(8,128)(2,1)S(1)} %broadcast_select_fusion.2), channel_id=1, source_target_pairs={{0,256},{256,512},{512,768},{1,257},{257,513},{513,769},{2,258},{2... | collective-permute-start | bytes 86024 | tf_op jit(solution)/shard_map/while/body/eval_jaxpr/ppermute | solution.py:56
  254.0 23.2 %all-to-all-start.3 = ((bf16[32,3,896]{2,1,0:T(4,128)(2,1)}), bf16[32,3,896]{2,1,0:T(4,128)(2,1)S(1)}, u32[]{:S(2)}, u32[]{:S(2)}) async-start(bf16[32,3,896]{2,1,0:T(4,128)(2,1)} %all_to_all.60), calls=%async_computation.3 | async-start | bytes 458752 | tf_op jit(solution)/shard_map/while/body/eval_jaxpr/all_to_all | solution.py:128
  278.8 16.2 %collective-permute-start = (bf16[16,896]{1,0:T(8,128)(2,1)S(1)}, bf16[16,896]{1,0:T(8,128)(2,1)S(1)}, u32[]{:S(2)}, u32[]{:S(2)}) collective-permute-start(bf16[16,896]{1,0:T(8,128)(2,1)S(1)} %broadcast_select_fusion.2), channel_id=1, source_target_pairs={{0,256},{256,512},{512,768},{1,257},{257,513},{513,769},{2,258},{2... | collective-permute-start | bytes 86024 | tf_op jit(solution)/shard_map/while/body/eval_jaxpr/ppermute | solution.py:56
  341.2 23.2 %all-to-all-start.3 = ((bf16[32,3,896]{2,1,0:T(4,128)(2,1)}), bf16[32,3,896]{2,1,0:T(4,128)(2,1)S(1)}, u32[]{:S(2)}, u32[]{:S(2)}) async-start(bf16[32,3,896]{2,1,0:T(4,128)(2,1)} %all_to_all.60), calls=%async_computation.3 | async-start | bytes 458752 | tf_op jit(solution)/shard_map/while/body/eval_jaxpr/all_to_all | solution.py:128
  366.0 16.2 %collective-permute-start = (bf16[16,896]{1,0:T(8,128)(2,1)S(1)}, bf16[16,896]{1,0:T(8,128)(2,1)S(1)}, u32[]{:S(2)}, u32[]{:S(2)}) collective-permute-start(bf16[16,896]{1,0:T(8,128)(2,1)S(1)} %broadcast_select_fusion.2), channel_id=1, source_target_pairs={{0,256},{256,512},{512,768},{1,257},{257,513},{513,769},{2,258},{2... | collective-permute-start | bytes 86024 | tf_op jit(solution)/shard_map/while/body/eval_jaxpr/ppermute | solution.py:56
  428.5 23.2 %all-to-all-start.3 = ((bf16[32,3,896]{2,1,0:T(4,128)(2,1)}), bf16[32,3,896]{2,1,0:T(4,128)(2,1)S(1)}, u32[]{:S(2)}, u32[]{:S(2)}) async-start(bf16[32,3,896]{2,1,0:T(4,128)(2,1)} %all_to_all.60), calls=%async_computation.3 | async-start | bytes 458752 | tf_op jit(solution)/shard_map/while/body/eval_jaxpr/all_to_all | solution.py:128
  453.3 16.2 %collective-permute-start = (bf16[16,896]{1,0:T(8,128)(2,1)S(1)}, bf16[16,896]{1,0:T(8,128)(2,1)S(1)}, u32[]{:S(2)}, u32[]{:S(2)}) collective-permute-start(bf16[16,896]{1,0:T(8,128)(2,1)S(1)} %broadcast_select_fusion.2), channel_id=1, source_target_pairs={{0,256},{256,512},{512,768},{1,257},{257,513},{513,769},{2,258},{2... | collective-permute-start | bytes 86024 | tf_op jit(solution)/shard_map/while/body/eval_jaxpr/ppermute | solution.py:56
  515.8 23.2 %all-to-all-start.3 = ((bf16[32,3,896]{2,1,0:T(4,128)(2,1)}), bf16[32,3,896]{2,1,0:T(4,128)(2,1)S(1)}, u32[]{:S(2)}, u32[]{:S(2)}) async-start(bf16[32,3,896]{2,1,0:T(4,128)(2,1)} %all_to_all.60), calls=%async_computation.3 | async-start | bytes 458752 | tf_op jit(solution)/shard_map/while/body/eval_jaxpr/all_to_all | solution.py:128
  540.5 16.2 %collective-permute-start = (bf16[16,896]{1,0:T(8,128)(2,1)S(1)}, bf16[16,896]{1,0:T(8,128)(2,1)S(1)}, u32[]{:S(2)}, u32[]{:S(2)}) collective-permute-start(bf16[16,896]{1,0:T(8,128)(2,1)S(1)} %broadcast_select_fusion.2), channel_id=1, source_target_pairs={{0,256},{256,512},{512,768},{1,257},{257,513},{513,769},{2,258},{2... | collective-permute-start | bytes 86024 | tf_op jit(solution)/shard_map/while/body/eval_jaxpr/ppermute | solution.py:56
  603.0 23.2 %all-to-all-start.3 = ((bf16[32,3,896]{2,1,0:T(4,128)(2,1)}), bf16[32,3,896]{2,1,0:T(4,128)(2,1)S(1)}, u32[]{:S(2)}, u32[]{:S(2)}) async-start(bf16[32,3,896]{2,1,0:T(4,128)(2,1)} %all_to_all.60), calls=%async_computation.3 | async-start | bytes 458752 | tf_op jit(solution)/shard_map/while/body/eval_jaxpr/all_to_all | solution.py:128
where the time goes:
time: 630 us; the launch traced here: 628 us
  blocking collectives  312 us (50%)
  starting transfers between devices  140 us (22%)
  waiting for transfers between devices  122 us (19%)
  local copies, waits for them, and re-layouts  23.6 us (4%)
  matrix products  18 us (3%)
  other arithmetic  11.8 us (2%)
    all_to_all x7, blocking collectives, run_layer(): lax.all_to_all(sent, 'expert', split_axis=0, concat_axis=0, tiled=True)  169 us
    all_to_all x7, waiting for transfers between devices, run_layer(): lax.all_to_all(outgoing, 'expert', split_axis=0, concat_axis=0, tiled=True)  119 us
    ppermute x7, starting transfers between devices, shifted(): lax.ppermute(value, axis, [(source, source + steps) for source in range(f...  102 us
    all_to_all x7, blocking collectives, sum_at_owner(): lax.all_to_all(parts, axis, split_axis=0, concat_axis=0, tiled=True)  83.7 us
    all_to_all x7, blocking collectives, copy_for_each(): return lax.all_to_all(copies, axis, split_axis=0, concat_axis=0, tiled=True)  59.4 us
    all_to_all x7, starting transfers between devices, run_layer(): lax.all_to_all(outgoing, 'expert', split_axis=0, concat_axis=0, tiled=True)  37.6 us
  transfers between devices with their start and end apart: 14, of which 14 were waited for; matrix products, arithmetic and copies ran while one was open for 2% of the time, Pallas kernels for 0%

commit v1 on v0

v1 whole, which is shorter than its diff:
```python
import functools

import jax
import jax.numpy as jnp
from jax import lax
from jax.experimental import pallas as pl
from jax.experimental.pallas import tpu as pltpu
from jax.sharding import PartitionSpec as P

D = 7168
CAP = 3
PAD = 4
NX = 4
EPS = 1e-06
STAGE_TIMES = (0.0, 9.0, 13.0, 18.0, 22.0, 26.0, 36.0)
SPACING = 18.0
MESH = pl.DeviceIdType.MESH


def schedule(micro):
    steps = [
        (start + SPACING * m, m, stage) for m in range(micro) for stage, start in enumerate(STAGE_TIMES)
    ]
    return [(m, stage) for _, m, stage in sorted(steps)]


def relay_kernel(
    sizes,
    tok_ref,
    w_in_ref,
    w_out_ref,
    place_ref,
    comb_ref,
    out_ref,
    x_in,
    z_out,
    z_in,
    x_got,
    h_out,
    h_in,
    acts,
    o_rows,
    r_in,
    f_out,
    f_in,
    send_sem,
    recv_sem,
):
    ns, nz, nh, micro = sizes
    s = lax.axis_index("section")
    e = lax.axis_index("expert")
    h = lax.axis_index("hidden")
    z = e // NX
    x = e % NX
    width = w_in_ref.shape[0]
    units = w_out_ref.shape[0]
    rows = NX * nz * PAD
    chunk = rows // nh

    def z_peer(k):
        return lax.rem(z + k, nz)

    def x_peer(k):
        return lax.rem(x + k, NX)

    def h_peer(k):
        return lax.rem(h + k, nh)

    def z_dev(zz):
        return {"expert": zz * NX + x}

    def x_dev(xx):
        return {"expert": z * NX + xx}

    barrier = pltpu.get_barrier_semaphore()

    def greet(axis_device):
        pl.semaphore_signal(barrier, inc=1, device_id=axis_device, device_id_type=MESH)

    @pl.loop(1, nz)
    def _(k):
        greet(z_dev(z_peer(k)))

    @pl.loop(1, NX)
    def _(k):
        greet(x_dev(x_peer(k)))

    @pl.loop(1, nh)
    def _(k):
        greet({"hidden": h_peer(k)})

    greet({"section": lax.rem(s + 1, ns)})
    greet({"section": lax.rem(s + ns - 1, ns)})
    pl.semaphore_wait(barrier, (nz - 1) + (NX - 1) + (nh - 1) + 2)

    def send(phase, m, src, dst, device):
        pltpu.make_async_remote_copy(
            src_ref=src,
            dst_ref=dst,
            send_sem=send_sem.at[phase, m],
            recv_sem=recv_sem.at[phase, m],
            device_id=device,
            device_id_type=MESH,
        ).start()

    def wait_bytes(sem, ref):
        pltpu.make_async_copy(ref, ref, sem).wait()

    def stage_a(m):
        @pl.when(s == 0)
        def _():
            x_in[m] = tok_ref[m]

        @pl.when(s > 0)
        def _():
            wait_bytes(recv_sem.at[6, m], x_in.at[m])

        slots = jnp.dot(place_ref[m], x_in[m], preferred_element_type=jnp.float32)
        z_out[m] = slots.astype(jnp.bfloat16).reshape(2, nz, PAD, width)

        @pl.loop(1, nz)
        def _(k):
            zz = z_peer(k)
            send(0, m, z_out.at[m, :, zz], z_in.at[m, :, z], z_dev(zz))

        z_in[m, :, z] = z_out[m, :, z]

    def stage_b(m):
        wait_bytes(recv_sem.at[0, m], z_in.at[m, :, pl.ds(0, nz - 1)])

        @pl.loop(1, NX)
        def _(k):
            xx = x_peer(k)
            send(1, m, z_in.at[m, xx // 2], x_got.at[m, x], x_dev(xx))

        x_got[m, x] = z_in[m, x // 2]

    def stage_c(m):
        wait_bytes(recv_sem.at[1, m], x_got.at[m, pl.ds(0, NX - 1)])
        held = x_got[m].reshape(rows, width)
        wide = held.astype(jnp.float32)
        squares = jnp.sum(wide * wide, axis=1, keepdims=True)
        h_out[m, :, :, 2 * units :] = (
            jnp.broadcast_to(squares, (rows, 128)).astype(jnp.bfloat16).reshape(nh, chunk, 128)
        )
        h_out[m, :, :, : 2 * units] = (
            jnp.dot(held, w_in_ref[...], preferred_element_type=jnp.float32)
            .astype(jnp.bfloat16)
            .reshape(nh, chunk, 2 * units)
        )

        @pl.loop(1, nh)
        def _(k):
            hh = h_peer(k)
            send(2, m, h_out.at[m, hh], h_in.at[m, h], {"hidden": hh})

        h_in[m, h] = h_out[m, h]

    def stage_d(m):
        wait_bytes(recv_sem.at[2, m], h_in.at[m, pl.ds(0, nh - 1)])
        total = h_in[m, 0].astype(jnp.float32)
        for k in range(1, nh):
            total = total + h_in[m, k].astype(jnp.float32)
        scale = lax.rsqrt(total[:, 2 * units : 2 * units + 1] / (width * nh) + EPS)
        gate = scale * total[:, :units]
        up = scale * total[:, units : 2 * units]
        acts[m, h] = (gate / (1.0 + jnp.exp(-gate)) * up).astype(jnp.bfloat16)

        @pl.loop(1, nh)
        def _(k):
            send(3, m, acts.at[m, h], acts.at[m, h], {"hidden": h_peer(k)})

    def stage_e(m):
        wait_bytes(recv_sem.at[3, m], acts.at[m, pl.ds(0, nh - 1)])
        held = acts[m].reshape(rows, units)
        o_rows[m] = (
            jnp.dot(held, w_out_ref[...], preferred_element_type=jnp.float32)
            .astype(jnp.bfloat16)
            .reshape(NX, nz, PAD, width)
        )

        @pl.loop(1, NX)
        def _(k):
            xx = x_peer(k)
            send(4, m, o_rows.at[m, xx], r_in.at[m, x], x_dev(xx))

        r_in[m, x] = o_rows[m, x]

    def stage_f(m):
        wait_bytes(recv_sem.at[4, m], r_in.at[m, pl.ds(0, NX - 1)])
        for pair in range(2):
            both = r_in[m, 2 * pair].astype(jnp.float32) + r_in[m, 2 * pair + 1].astype(jnp.float32)
            f_out[m, pair] = both.astype(jnp.bfloat16)

        @pl.loop(1, nz)
        def _(k):
            zz = z_peer(k)
            send(5, m, f_out.at[m, :, zz], f_in.at[m, :, z], z_dev(zz))

        f_in[m, :, z] = f_out[m, :, z]

    def stage_g(m):
        wait_bytes(recv_sem.at[5, m], f_in.at[m, :, pl.ds(0, nz - 1)])
        back = f_in[m].reshape(2 * nz * PAD, width)
        mixed = jnp.dot(comb_ref[m], back, preferred_element_type=jnp.float32)
        out_ref[m] = (x_in[m].astype(jnp.float32) + mixed).astype(jnp.bfloat16)

        @pl.when(s < ns - 1)
        def _():
            send(6, m, out_ref.at[m], x_in.at[m], {"section": s + 1})

    stages = (stage_a, stage_b, stage_c, stage_d, stage_e, stage_f, stage_g)
    for m, stage in schedule(micro):
        stages[stage](m)

    for m in range(micro):
        wait_bytes(send_sem.at[0, m], z_out.at[m, :, pl.ds(0, nz - 1)])
        wait_bytes(send_sem.at[1, m], x_got.at[m, pl.ds(0, NX - 1)])
        wait_bytes(send_sem.at[2, m], h_out.at[m, pl.ds(0, nh - 1)])
        wait_bytes(send_sem.at[3, m], acts.at[m, pl.ds(0, nh - 1)])
        wait_bytes(send_sem.at[4, m], o_rows.at[m, pl.ds(0, NX - 1)])
        wait_bytes(send_sem.at[5, m], f_out.at[m, :, pl.ds(0, nz - 1)])

        @pl.when(s < ns - 1)
        def _():
            wait_bytes(send_sem.at[6, m], out_ref.at[m])


def tables(routes, gate_weights, nz):
    ids = 2 * jnp.arange(nz, dtype=jnp.int32)[None, :] + jnp.arange(2, dtype=jnp.int32)[:, None]
    ids = ids.reshape(2 * nz)
    matches = routes[:, :, :, None] == ids
    chosen = jnp.sum(matches.astype(jnp.int32), axis=2, dtype=jnp.int32)
    weight = jnp.sum(
        jnp.where(matches, gate_weights.astype(jnp.float32)[:, :, :, None], jnp.float32(0.0)), axis=2
    )
    rank = jnp.cumsum(chosen, axis=1, dtype=jnp.int32) - chosen
    caps = jnp.arange(PAD, dtype=jnp.int32)
    hits = (rank[..., None] == caps) & (chosen[..., None] == 1) & (caps < CAP)
    micro, toks = routes.shape[:2]
    hits = hits.reshape(micro, toks, 2 * nz * PAD).astype(jnp.float32)
    comb = hits * jnp.repeat(weight, PAD, axis=2)
    place = hits.transpose(0, 2, 1)
    return place.astype(jnp.bfloat16), comb.astype(jnp.bfloat16)


def on_device(tokens, gate_up, down_proj, routes, gate_weights):
    ns = lax.axis_size("section")
    nz = lax.axis_size("expert") // NX
    nh = lax.axis_size("hidden")
    micro, toks, width = tokens.shape
    units = down_proj.shape[1]
    rows = NX * nz * PAD
    chunk = rows // nh
    w_in = gate_up[0].reshape(width, 2 * units)
    w_out = down_proj[0]
    place, comb = tables(routes[0], gate_weights[0], nz)
    vmem = pl.BlockSpec(memory_space=pltpu.VMEM)
    bf16 = jnp.bfloat16
    out = pl.pallas_call(
        functools.partial(relay_kernel, (ns, nz, nh, micro)),
        out_shape=jax.ShapeDtypeStruct((micro, toks, width), bf16),
        in_specs=[vmem] * 5,
        out_specs=vmem,
        scratch_shapes=[
            pltpu.VMEM((micro, toks, width), bf16),
            pltpu.VMEM((micro, 2, nz, PAD, width), bf16),
            pltpu.VMEM((micro, 2, nz, PAD, width), bf16),
            pltpu.VMEM((micro, NX, nz, PAD, width), bf16),
            pltpu.VMEM((micro, nh, chunk, 2 * units + 128), bf16),
            pltpu.VMEM((micro, nh, chunk, 2 * units + 128), bf16),
            pltpu.VMEM((micro, nh, chunk, units), bf16),
            pltpu.VMEM((micro, NX, nz, PAD, width), bf16),
            pltpu.VMEM((micro, NX, nz, PAD, width), bf16),
            pltpu.VMEM((micro, 2, nz, PAD, width), bf16),
            pltpu.VMEM((micro, 2, nz, PAD, width), bf16),
            pltpu.SemaphoreType.DMA((7, micro)),
            pltpu.SemaphoreType.DMA((7, micro)),
        ],
        compiler_params=pltpu.CompilerParams(
            collective_id=0, has_side_effects=True, vmem_limit_bytes=40 << 20
        ),
        name="relay",
    )(tokens, w_in, w_out, place, comb)
    return out[None]


def solution(mesh):
    placed = (
        P(None, "expert", "hidden"),
        P("section", "hidden", None, "expert"),
        P("section", "expert", "hidden"),
        P("section", None, "expert", None),
        P("section", None, "expert", None),
    )
    return jax.shard_map(
        on_device,
        mesh=mesh,
        in_specs=placed,
        out_specs=P("section", None, "expert", "hidden"),
        check_vma=False,
    )
```

time: 630 us -> 240 us (0.38)
  the two profiles are of different devices: /device:TPU:8 before, /device:TPU:992 now
where the time goes in v1:
time: 240 us
  Pallas kernels  233 us (97%)
  local copies, waits for them, and re-layouts  3.69 us (2%)
    pallas_call x1, Pallas kernels, on_device(): pl.pallas_call(functools.partial(relay_kernel, (ns, nz, nh, micro)), out_...  233 us

profile of v1, /device:TPU:992, one launch (start us, length us, event | category | flops | bytes accessed | tf_op | source)
XLA Modules:
  0.0 239.5 jit_solution(15758702181420856429)
XLA Ops:
  0.0 0.1 add.23
  0.1 0.1 and.28
  0.2 0.7 bitcast_convert_fusion
  0.9 0.1 eq.53
  1.0 0.8 fusion.1
  1.8 0.1 copy.29
  1.9 0.8 fusion
  2.7 0.1 copy.25
  2.8 0.1 copy.26
  2.9 0.1 reduce_window_sum.11
  3.0 0.1 copy.23
  3.1 0.1 copy.30
  3.2 0.1 copy.24
  3.3 0.1 copy.31.place_ref
  3.4 0.0 copy-start
  3.4 0.0 copy-start.1
  3.4 2.1 copy.34
  5.5 0.0 copy-done
  5.5 0.0 copy-done.1
  5.5 233.3 %relay.1 = bf16[4,16,896]{2,1,0:T(8,128)(2,1)S(1)} custom-call(bf16[4,16,896]{2,1,0:T(8,128)(2,1)S(1)} %copy-done.1, bf16[896,1024]{1,0:T(8,128)(2,1)S(1)} %bitcast.14, bf16[512,896]{1,0:T(8,128)(2,1)S(1)} %bitcast.15, bf16[4,64,16]{2,1,0:T(8,128)(2,1)S(1)} %copy.31.place_ref, bf16[4,16,64]{2,1,0:T(8,128)(2,1)S(1)} %get-tuple-element.5.comb_ref), custom_call_target="tpu_custom_call" | custom-call | tf_op jit(solution)/shard_map/relay/pallas_call | solution.py:260
  238.9 0.6 copy.36
  (12 shorter events, 0.2 us)
Async XLA Ops:
  3.4 2.1 copy-start
  3.4 2.1 copy-start.1

commit v2 on v1

--- a/solution.py
+++ b/solution.py
@@ -12,9 +12,28 @@
 PAD = 4
 NX = 4
 EPS = 1e-06
-STAGE_TIMES = (0.0, 9.0, 13.0, 18.0, 22.0, 26.0, 36.0)
-SPACING = 18.0
+STAGE_TIMES = (0.0, 7.5, 12.1, 17.7, 23.1, 27.7, 35.2)
+SPACING = 8.5
 MESH = pl.DeviceIdType.MESH
+
+
+def tables(nz, route, gate, hit_ref, comb_ref):
+    toks = route.shape[0]
+    slots = 2 * nz * PAD
+    lane = lax.broadcasted_iota(jnp.int32, (toks, slots), 1)
+    expert = 2 * (lane // PAD % nz) + lane // (PAD * nz)
+    cap = lane % PAD
+    first, second = route[:, 0:1] == expert, route[:, 1:2] == expert
+    chosen = jnp.where(first | second, 1.0, 0.0)
+    row = lax.broadcasted_iota(jnp.int32, (toks, toks), 0)
+    col = lax.broadcasted_iota(jnp.int32, (toks, toks), 1)
+    before = jnp.where(col < row, 1.0, 0.0).astype(jnp.bfloat16)
+    rank = jnp.dot(before, chosen.astype(jnp.bfloat16), preferred_element_type=jnp.float32)
+    hit = jnp.where((rank == cap.astype(jnp.float32)) & (cap < CAP), chosen, 0.0)
+    wide = gate.astype(jnp.float32)
+    weight = jnp.where(first, wide[:, 0:1], 0.0) + jnp.where(second, wide[:, 1:2], 0.0)
+    hit_ref[...] = hit.astype(jnp.bfloat16)
+    comb_ref[...] = (hit * weight).astype(jnp.bfloat16)
 
 
 def schedule(micro):
@@ -29,9 +48,11 @@
     tok_ref,
     w_in_ref,
     w_out_ref,
-    place_ref,
+    route_ref,
+    gate_ref,
+    out_ref,
+    hit_ref,
     comb_ref,
-    out_ref,
     x_in,
     z_out,
     z_in,
@@ -45,6 +66,8 @@
     f_in,
     send_sem,
     recv_sem,
+    ready_sem,
+    z_sem,
 ):
     ns, nz, nh, micro = sizes
     s = lax.axis_index("section")
@@ -60,6 +83,9 @@
     def z_peer(k):
         return lax.rem(z + k, nz)
 
+    def ends(far):
+        return ((z + far, z + far < nz), (z - far, z - far >= 0))
+
     def x_peer(k):
         return lax.rem(x + k, NX)
 
@@ -76,6 +102,10 @@
 
     def greet(axis_device):
         pl.semaphore_signal(barrier, inc=1, device_id=axis_device, device_id_type=MESH)
+
+    @pl.when(s < ns - 1)
+    def _():
+        greet({"section": s + 1})
 
     @pl.loop(1, nz)
     def _(k):
@@ -89,16 +119,26 @@
     def _(k):
         greet({"hidden": h_peer(k)})
 
-    greet({"section": lax.rem(s + 1, ns)})
-    greet({"section": lax.rem(s + ns - 1, ns)})
-    pl.semaphore_wait(barrier, (nz - 1) + (NX - 1) + (nh - 1) + 2)
-
-    def send(phase, m, src, dst, device):
+    for m in range(micro):
+        tables(nz, route_ref[m], gate_ref[m], hit_ref.at[m], comb_ref.at[m])
+    near = (nz - 1) + (NX - 1) + (nh - 1)
+
+    @pl.when(s == 0)
+    def _():
+        pl.semaphore_wait(barrier, near)
+
+    @pl.when(s > 0)
+    def _():
+        pl.semaphore_wait(barrier, near + 1)
+        pl.semaphore_signal(ready_sem, inc=1, device_id={"section": s - 1}, device_id_type=MESH)
+
+
+    def send(phase, m, src, dst, device, arrive=None):
         pltpu.make_async_remote_copy(
             src_ref=src,
             dst_ref=dst,
             send_sem=send_sem.at[phase, m],
-            recv_sem=recv_sem.at[phase, m],
+            recv_sem=recv_sem.at[phase, m] if arrive is None else arrive,
             device_id=device,
             device_id_type=MESH,
         ).start()
@@ -115,23 +155,37 @@
         def _():
             wait_bytes(recv_sem.at[6, m], x_in.at[m])
 
-        slots = jnp.dot(place_ref[m], x_in[m], preferred_element_type=jnp.float32)
+        slots = lax.dot_general(
+            hit_ref[m], x_in[m], (((0,), (0,)), ((), ())), preferred_element_type=jnp.float32
+        )
         z_out[m] = slots.astype(jnp.bfloat16).reshape(2, nz, PAD, width)
 
+        @pl.loop(0, nz - 1)
+        def _(k):
+            for zz, there in ends(nz - 1 - k):
+                @pl.when(there)
+                def _():
+                    send(0, m, z_out.at[m, :, zz], z_in.at[m, :, z], z_dev(zz), z_sem.at[m, z])
+
+        z_in[m, :, z] = z_out[m, :, z]
+
+    def stage_b(m):
+        def forward(zz):
+            @pl.loop(1, NX)
+            def _(k):
+                xx = x_peer(k)
+                send(1, m, z_in.at[m, xx // 2, zz], x_got.at[m, x, zz], x_dev(xx))
+
+        forward(z)
+
         @pl.loop(1, nz)
-        def _(k):
-            zz = z_peer(k)
-            send(0, m, z_out.at[m, :, zz], z_in.at[m, :, z], z_dev(zz))
-
-        z_in[m, :, z] = z_out[m, :, z]
-
-    def stage_b(m):
-        wait_bytes(recv_sem.at[0, m], z_in.at[m, :, pl.ds(0, nz - 1)])
-
-        @pl.loop(1, NX)
-        def _(k):
-            xx = x_peer(k)
-            send(1, m, z_in.at[m, xx // 2], x_got.at[m, x], x_dev(xx))
+        def _(far):
+            for zz, there in ends(far):
+
+                @pl.when(there)
+                def _():
+                    wait_bytes(z_sem.at[m, zz], z_in.at[m, :, 0])
+                    forward(zz)
 
         x_got[m, x] = z_in[m, x // 2]
 
@@ -192,10 +246,12 @@
             both = r_in[m, 2 * pair].astype(jnp.float32) + r_in[m, 2 * pair + 1].astype(jnp.float32)
             f_out[m, pair] = both.astype(jnp.bfloat16)
 
-        @pl.loop(1, nz)
-        def _(k):
-            zz = z_peer(k)
-            send(5, m, f_out.at[m, :, zz], f_in.at[m, :, z], z_dev(zz))
+        @pl.loop(0, nz - 1)
+        def _(k):
+            for zz, there in ends(nz - 1 - k):
+                @pl.when(there)
+                def _():
+                    send(5, m, f_out.at[m, :, zz], f_in.at[m, :, z], z_dev(zz))
 
         f_in[m, :, z] = f_out[m, :, z]
 
@@ -207,6 +263,8 @@
 
         @pl.when(s < ns - 1)
         def _():
+            if m == 0:
+                pl.semaphore_wait(ready_sem, 1)
             send(6, m, out_ref.at[m], x_in.at[m], {"section": s + 1})
 
     stages = (stage_a, stage_b, stage_c, stage_d, stage_e, stage_f, stage_g)
@@ -224,24 +282,6 @@
         @pl.when(s < ns - 1)
         def _():
             wait_bytes(send_sem.at[6, m], out_ref.at[m])
-
-
-def tables(routes, gate_weights, nz):
-    ids = 2 * jnp.arange(nz, dtype=jnp.int32)[None, :] + jnp.arange(2, dtype=jnp.int32)[:, None]
-    ids = ids.reshape(2 * nz)
-    matches = routes[:, :, :, None] == ids
-    chosen = jnp.sum(matches.astype(jnp.int32), axis=2, dtype=jnp.int32)
-    weight = jnp.sum(
-        jnp.where(matches, gate_weights.astype(jnp.float32)[:, :, :, None], jnp.float32(0.0)), axis=2
-    )
-    rank = jnp.cumsum(chosen, axis=1, dtype=jnp.int32) - chosen
-    caps = jnp.arange(PAD, dtype=jnp.int32)
-    hits = (rank[..., None] == caps) & (chosen[..., None] == 1) & (caps < CAP)
-    micro, toks = routes.shape[:2]
-    hits = hits.reshape(micro, toks, 2 * nz * PAD).astype(jnp.float32)
-    comb = hits * jnp.repeat(weight, PAD, axis=2)
-    place = hits.transpose(0, 2, 1)
-    return place.astype(jnp.bfloat16), comb.astype(jnp.bfloat16)
 
 
 def on_device(tokens, gate_up, down_proj, routes, gate_weights):
@@ -254,7 +294,6 @@
     chunk = rows // nh
     w_in = gate_up[0].reshape(width, 2 * units)
     w_out = down_proj[0]
-    place, comb = tables(routes[0], gate_weights[0], nz)
     vmem = pl.BlockSpec(memory_space=pltpu.VMEM)
     bf16 = jnp.bfloat16
     out = pl.pallas_call(
@@ -263,6 +302,8 @@
         in_specs=[vmem] * 5,
         out_specs=vmem,
         scratch_shapes=[
+            pltpu.VMEM((micro, toks, 2 * nz * PAD), bf16),
+            pltpu.VMEM((micro, toks, 2 * nz * PAD), bf16),
             pltpu.VMEM((micro, toks, width), bf16),
             pltpu.VMEM((micro, 2, nz, PAD, width), bf16),
             pltpu.VMEM((micro, 2, nz, PAD, width), bf16),
@@ -276,12 +317,14 @@
             pltpu.VMEM((micro, 2, nz, PAD, width), bf16),
             pltpu.SemaphoreType.DMA((7, micro)),
             pltpu.SemaphoreType.DMA((7, micro)),
+            pltpu.SemaphoreType.REGULAR,
+            pltpu.SemaphoreType.DMA((micro, nz)),
         ],
         compiler_params=pltpu.CompilerParams(
             collective_id=0, has_side_effects=True, vmem_limit_bytes=40 << 20
         ),
         name="relay",
-    )(tokens, w_in, w_out, place, comb)
+    )(tokens, w_in, w_out, routes[0], gate_weights[0])
     return out[None]
 
 

time: 240 us -> 213 us (0.89)
  Pallas kernels: 233 us -> 207 us
    pallas_call x1, Pallas kernels: 233 us -> 207 us  [on_device(): pl.pallas_call(functools.partial(relay_kernel, (ns, nz, nh, micro)), out_...]
where the time goes in v2:
time: 213 us; the launch traced here: 212 us
  Pallas kernels  207 us (97%)
  local copies, waits for them, and re-layouts  4.3 us (2%)
    pallas_call x1, Pallas kernels, on_device(): pl.pallas_call(functools.partial(relay_kernel, (ns, nz, nh, micro)), out_...  207 us

profile of v2, /device:TPU:992, one launch (start us, length us, event | category | flops | bytes accessed | tf_op | source)
XLA Modules:
  0.0 211.6 jit_solution(4077375248894294956)
XLA Ops:
  0.0 0.8 copy.9.gate_ref
  0.8 0.8 copy.8.route_ref
  1.6 0.0 copy-start
  1.6 0.0 copy-start.1
  1.6 2.1 copy.14
  3.7 0.0 copy-done
  3.7 0.0 copy-done.1
  3.7 207.2 %relay.1 = bf16[4,16,896]{2,1,0:T(8,128)(2,1)S(1)} custom-call(bf16[4,16,896]{2,1,0:T(8,128)(2,1)S(1)} %copy-done.1, bf16[896,1024]{1,0:T(8,128)(2,1)S(1)} %bitcast.7, bf16[512,896]{1,0:T(8,128)(2,1)S(1)} %bitcast.8, s32[4,16,2]{2,1,0:T(8,128)S(1)} %copy.8.route_ref, bf16[4,16,2]{2,1,0:T(8,128)(2,1)S(1)} %copy.9.gate_ref), custom_call_target="tpu_custom_call" | custom-call | tf_op jit(solution)/shard_map/relay/pallas_call | solution.py:299
  210.9 0.6 copy.16
Async XLA Ops:
  1.6 2.1 copy-start
  1.6 2.1 copy-start.1

commit v3 on v2

v3 whole, which is shorter than its diff:
```python
import functools

import jax
import jax.numpy as jnp
from jax import lax
from jax.experimental import pallas as pl
from jax.experimental.pallas import tpu as pltpu
from jax.sharding import PartitionSpec as P

D = 7168
CAP = 3
PAD = 4
NX = 4
EPS = 1e-06
ORDER = (
    0, 1, 10, 2, 3, 11, 4, 20,
    12, 5, 13, 6, 21, 14, 30, 22,
    15, 7, 23, 16, 31, 24, 32, 25,
    17, 33, 26, 34, 35, 27, 36, 37,
)
MESH = pl.DeviceIdType.MESH


def tables(nz, route, gate, hit_ref, comb_ref):
    toks = route.shape[0]
    slots = 2 * nz * CAP
    lane = lax.broadcasted_iota(jnp.int32, (toks, slots), 1)
    expert = 2 * (lane // (2 * CAP)) + lane % 2
    cap = lane % (2 * CAP) // 2
    first, second = route[:, 0:1] == expert, route[:, 1:2] == expert
    chosen = jnp.where(first | second, 1.0, 0.0)
    row = lax.broadcasted_iota(jnp.int32, (toks, toks), 0)
    col = lax.broadcasted_iota(jnp.int32, (toks, toks), 1)
    before = jnp.where(col < row, 1.0, 0.0).astype(jnp.bfloat16)
    rank = jnp.dot(before, chosen.astype(jnp.bfloat16), preferred_element_type=jnp.float32)
    hit = jnp.where(rank == cap.astype(jnp.float32), chosen, 0.0)
    wide = gate.astype(jnp.float32)
    weight = jnp.where(first, wide[:, 0:1], 0.0) + jnp.where(second, wide[:, 1:2], 0.0)
    hit_ref[...] = hit.astype(jnp.bfloat16)
    comb_ref[...] = (hit * weight).astype(jnp.bfloat16)


def regroupings(nz, to_x_ref, to_z_ref):
    slots, group = 2 * nz * CAP, nz * CAP
    r = lax.broadcasted_iota(jnp.int32, (slots, slots), 0)
    j = lax.broadcasted_iota(jnp.int32, (slots, slots), 1)
    source = 2 * (r % group) + r // group
    to_x_ref[...] = jnp.where(source == j, 1.0, 0.0).astype(jnp.bfloat16)
    r = lax.broadcasted_iota(jnp.int32, (slots, NX * group), 1)
    j = lax.broadcasted_iota(jnp.int32, (slots, NX * group), 0)
    target = 2 * (r % group) + r // (2 * group)
    to_z_ref[...] = jnp.where(target == j, 1.0, 0.0).astype(jnp.bfloat16)


def relay_kernel(
    sizes,
    tok_ref,
    w_in_ref,
    w_out_ref,
    route_ref,
    gate_ref,
    out_ref,
    hit_ref,
    comb_ref,
    to_x_ref,
    to_z_ref,
    x_in,
    z_out,
    z_in,
    x_out,
    x_got,
    p_out,
    p_in,
    y_out,
    y_in,
    acts,
    o_rows,
    r_in,
    f_out,
    f_in,
    send_sem,
    recv_sem,
    ready_sem,
):
    ns, nz, nh, micro = sizes
    ny = nh // 2
    s = lax.axis_index("section")
    e = lax.axis_index("expert")
    h = lax.axis_index("hidden")
    z = e // NX
    x = e % NX
    y = h // 2
    core = h % 2
    width = w_in_ref.shape[0]
    units = w_out_ref.shape[0]
    half = units // 2
    slots = 2 * nz * CAP
    group = nz * CAP
    rows = NX * group
    chunk = rows // ny

    def ends(far):
        return ((z + far, z + far < nz), (z - far, z - far >= 0))

    def x_peer(k):
        return lax.rem(x + k, NX)

    def y_peer(k):
        return lax.rem(y + k, ny)

    def h_peer(k):
        return lax.rem(h + k, nh)

    def z_dev(zz):
        return {"expert": zz * NX + x}

    def x_dev(xx):
        return {"expert": z * NX + xx}

    barrier = pltpu.get_barrier_semaphore()

    def greet(axis_device):
        pl.semaphore_signal(barrier, inc=1, device_id=axis_device, device_id_type=MESH)

    @pl.when(s < ns - 1)
    def _():
        greet({"section": s + 1})

    @pl.loop(1, nz)
    def _(k):
        greet(z_dev(lax.rem(z + k, nz)))

    @pl.loop(1, NX)
    def _(k):
        greet(x_dev(x_peer(k)))

    @pl.loop(1, nh)
    def _(k):
        greet({"hidden": h_peer(k)})

    for m in range(micro):
        tables(nz, route_ref[m], gate_ref[m], hit_ref.at[m], comb_ref.at[m])
    regroupings(nz, to_x_ref, to_z_ref)
    near = (nz - 1) + (NX - 1) + (nh - 1)

    @pl.when(s == 0)
    def _():
        pl.semaphore_wait(barrier, near)

    @pl.when(s > 0)
    def _():
        pl.semaphore_wait(barrier, near + 1)
        pl.semaphore_signal(ready_sem, inc=1, device_id={"section": s - 1}, device_id_type=MESH)

    def send(phase, m, src, dst, device):
        pltpu.make_async_remote_copy(
            src_ref=src,
            dst_ref=dst,
            send_sem=send_sem.at[phase, m],
            recv_sem=recv_sem.at[phase, m],
            device_id=device,
            device_id_type=MESH,
        ).start()

    def wait_bytes(sem, ref):
        pltpu.make_async_copy(ref, ref, sem).wait()

    def matmul(a, b):
        return jnp.dot(a, b, preferred_element_type=jnp.float32)

    def stage_a(m):
        @pl.when(s == 0)
        def _():
            x_in[m] = tok_ref[m]

        @pl.when(s > 0)
        def _():
            wait_bytes(recv_sem.at[7, m], x_in.at[m])

        picked = lax.dot_general(
            hit_ref[m], x_in[m], (((0,), (0,)), ((), ())), preferred_element_type=jnp.float32
        )
        z_out[m] = picked.astype(jnp.bfloat16).reshape(nz, CAP, 2, width)

        @pl.loop(0, nz - 1)
        def _(k):
            for zz, there in ends(nz - 1 - k):

                @pl.when(there)
                def _():
                    send(0, m, z_out.at[m, zz], z_in.at[m, z], z_dev(zz))

        z_in[m, z] = z_out[m, z]

    def stage_b(m):
        wait_bytes(recv_sem.at[0, m], z_in.at[m, pl.ds(0, nz - 1)])
        sorted_rows = matmul(to_x_ref[...], z_in[m].reshape(slots, width))
        x_out[m] = sorted_rows.astype(jnp.bfloat16).reshape(2, group, width)

        @pl.loop(1, NX)
        def _(k):
            xx = x_peer(k)
            send(1, m, x_out.at[m, xx // 2], x_got.at[m, x], x_dev(xx))

        x_got[m, x] = x_out[m, x // 2]

    def stage_c(m):
        wait_bytes(recv_sem.at[1, m], x_got.at[m, pl.ds(0, NX - 1)])
        held = x_got[m].reshape(rows, width)
        projected = matmul(held, w_in_ref[...]).astype(jnp.bfloat16)
        wide = held.astype(jnp.float32)
        squares = jnp.sum(wide * wide, axis=1, keepdims=True)
        spread = jnp.broadcast_to(squares, (rows, 128)).astype(jnp.bfloat16)
        for c in range(2):
            p_out[m, c, :, :half] = projected[:, c * half : (c + 1) * half]
            p_out[m, c, :, half:units] = projected[:, units + c * half : units + (c + 1) * half]
            p_out[m, c, :, units:] = spread
        send(2, m, p_out.at[m, 1 - core], p_in.at[m], {"hidden": 2 * y + 1 - core})

    def stage_d(m):
        wait_bytes(recv_sem.at[2, m], p_in.at[m])
        both = p_out[m, core].astype(jnp.float32) + p_in[m].astype(jnp.float32)
        y_out[m] = both.astype(jnp.bfloat16).reshape(ny, chunk, units + 128)

        @pl.loop(1, ny)
        def _(k):
            yy = y_peer(k)
            send(3, m, y_out.at[m, yy], y_in.at[m, y], {"hidden": 2 * yy + core})

        y_in[m, y] = y_out[m, y]

    def stage_e(m):
        wait_bytes(recv_sem.at[3, m], y_in.at[m, pl.ds(0, ny - 1)])
        total = y_in[m, 0].astype(jnp.float32)
        for k in range(1, ny):
            total = total + y_in[m, k].astype(jnp.float32)
        scale = lax.rsqrt(total[:, units : units + 1] / (width * nh) + EPS)
        gate = scale * total[:, :half]
        up = scale * total[:, half:units]
        mine = core * ny + y
        acts[m, mine] = (gate / (1.0 + jnp.exp(-gate)) * up).astype(jnp.bfloat16)

        @pl.loop(1, nh)
        def _(k):
            send(4, m, acts.at[m, mine], acts.at[m, mine], {"hidden": h_peer(k)})

    def stage_f(m):
        wait_bytes(recv_sem.at[4, m], acts.at[m, pl.ds(0, nh - 1)])
        low = acts[m, :ny].reshape(rows, half)
        high = acts[m, ny:].reshape(rows, half)
        made = matmul(low, w_out_ref[:half]) + matmul(high, w_out_ref[half:])
        o_rows[m] = made.astype(jnp.bfloat16).reshape(NX, group, width)

        @pl.loop(1, NX)
        def _(k):
            xx = x_peer(k)
            send(5, m, o_rows.at[m, xx], r_in.at[m, x], x_dev(xx))

        r_in[m, x] = o_rows[m, x]

    def stage_g(m):
        wait_bytes(recv_sem.at[5, m], r_in.at[m, pl.ds(0, NX - 1)])
        paired = matmul(to_z_ref[...], r_in[m].reshape(rows, width))
        f_out[m] = paired.astype(jnp.bfloat16).reshape(nz, CAP, 2, width)

        @pl.loop(0, nz - 1)
        def _(k):
            for zz, there in ends(nz - 1 - k):

                @pl.when(there)
                def _():
                    send(6, m, f_out.at[m, zz], f_in.at[m, z], z_dev(zz))

        f_in[m, z] = f_out[m, z]

    def stage_h(m):
        wait_bytes(recv_sem.at[6, m], f_in.at[m, pl.ds(0, nz - 1)])
        mixed = matmul(comb_ref[m], f_in[m].reshape(slots, width))
        out_ref[m] = (x_in[m].astype(jnp.float32) + mixed).astype(jnp.bfloat16)

        @pl.when(s < ns - 1)
        def _():
            if m == 0:
                pl.semaphore_wait(ready_sem, 1)
            send(7, m, out_ref.at[m], x_in.at[m], {"section": s + 1})

    stages = (stage_a, stage_b, stage_c, stage_d, stage_e, stage_f, stage_g, stage_h)
    for step in ORDER:
        m, stage = step // 10, step % 10
        if m < micro:
            stages[stage](m)

    for m in range(micro):
        wait_bytes(send_sem.at[0, m], z_out.at[m, pl.ds(0, nz - 1)])
        wait_bytes(send_sem.at[1, m], x_got.at[m, pl.ds(0, NX - 1)])
        wait_bytes(send_sem.at[2, m], p_in.at[m])
        wait_bytes(send_sem.at[3, m], y_out.at[m, pl.ds(0, ny - 1)])
        wait_bytes(send_sem.at[4, m], acts.at[m, pl.ds(0, nh - 1)])
        wait_bytes(send_sem.at[5, m], o_rows.at[m, pl.ds(0, NX - 1)])
        wait_bytes(send_sem.at[6, m], f_out.at[m, pl.ds(0, nz - 1)])

        @pl.when(s < ns - 1)
        def _():
            wait_bytes(send_sem.at[7, m], out_ref.at[m])


def on_device(tokens, gate_up, down_proj, routes, gate_weights):
    ns = lax.axis_size("section")
    nz = lax.axis_size("expert") // NX
    nh = lax.axis_size("hidden")
    ny = nh // 2
    micro, toks, width = tokens.shape
    units = down_proj.shape[1]
    slots, group = 2 * nz * CAP, nz * CAP
    rows = NX * group
    chunk = rows // ny
    w_in = gate_up[0].reshape(width, 2 * units)
    w_out = down_proj[0]
    vmem = pl.BlockSpec(memory_space=pltpu.VMEM)
    bf16 = jnp.bfloat16

    def held(*shape):
        return pltpu.VMEM((micro, *shape), bf16)

    out = pl.pallas_call(
        functools.partial(relay_kernel, (ns, nz, nh, micro)),
        out_shape=jax.ShapeDtypeStruct((micro, toks, width), bf16),
        in_specs=[vmem] * 5,
        out_specs=vmem,
        scratch_shapes=[
            held(toks, slots),
            held(toks, slots),
            pltpu.VMEM((slots, slots), bf16),
            pltpu.VMEM((slots, rows), bf16),
            held(toks, width),
            held(nz, CAP, 2, width),
            held(nz, CAP, 2, width),
            held(2, group, width),
            held(NX, group, width),
            held(2, rows, units + 128),
            held(rows, units + 128),
            held(ny, chunk, units + 128),
            held(ny, chunk, units + 128),
            held(nh, chunk, units // 2),
            held(NX, group, width),
            held(NX, group, width),
            held(nz, CAP, 2, width),
            held(nz, CAP, 2, width),
            pltpu.SemaphoreType.DMA((8, micro)),
            pltpu.SemaphoreType.DMA((8, micro)),
            pltpu.SemaphoreType.REGULAR,
        ],
        compiler_params=pltpu.CompilerParams(
            collective_id=0, has_side_effects=True, vmem_limit_bytes=40 << 20
        ),
        name="relay",
    )(tokens, w_in, w_out, routes[0], gate_weights[0])
    return out[None]


def solution(mesh):
    placed = (
        P(None, "expert", "hidden"),
        P("section", "hidden", None, "expert"),
        P("section", "expert", "hidden"),
        P("section", None, "expert", None),
        P("section", None, "expert", None),
    )
    return jax.shard_map(
        on_device,
        mesh=mesh,
        in_specs=placed,
        out_specs=P("section", None, "expert", "hidden"),
        check_vma=False,
    )
```

time: 213 us -> 198 us (0.930)
  Pallas kernels: 207 us -> 194 us
    pallas_call x1, Pallas kernels: 207 us -> 194 us  [on_device(): pl.pallas_call(functools.partial(relay_kernel, (ns, nz, nh, micro)), out_...]
where the time goes in v3:
time: 198 us
  Pallas kernels  194 us (98%)
  local copies, waits for them, and re-layouts  4.3 us (2%)
    pallas_call x1, Pallas kernels, on_device(): pl.pallas_call(functools.partial(relay_kernel, (ns, nz, nh, micro)), out_...  194 us

profile of v3, /device:TPU:992, one launch (start us, length us, event | category | flops | bytes accessed | tf_op | source)
XLA Modules:
  0.0 198.1 jit_solution(10700479742451806883)
XLA Ops:
  0.0 0.8 copy.9.gate_ref
  0.8 0.8 copy.8.route_ref
  1.6 0.0 copy-start
  1.6 0.0 copy-start.1
  1.6 2.1 %copy.14 = bf16[112,8,2,512]{3,1,2,0:T(8,128)(2,1)S(1)} copy(bf16[112,8,2,512]{3,2,1,0:T(2,128)(2,1)} %bitcast.10) | data formatting | bytes 3670016
  3.7 0.0 copy-done
  3.7 0.0 copy-done.1
  3.7 193.7 %relay.1 = bf16[4,16,896]{2,1,0:T(8,128)(2,1)S(1)} custom-call(bf16[4,16,896]{2,1,0:T(8,128)(2,1)S(1)} %copy-done.1, bf16[896,1024]{1,0:T(8,128)(2,1)S(1)} %bitcast.7, bf16[512,896]{1,0:T(8,128)(2,1)S(1)} %bitcast.8, s32[4,16,2]{2,1,0:T(8,128)S(1)} %copy.8.route_ref, bf16[4,16,2]{2,1,0:T(8,128)(2,1)S(1)} %copy.9.gate_ref), custom_call_target="tpu_custom_call" | custom-call | tf_op jit(solution)/shard_map/relay/pallas_call | solution.py:325
  197.4 0.6 copy.16
Async XLA Ops:
  1.6 2.1 %copy-start = (bf16[1,512,896]{2,1,0:T(8,128)(2,1)S(1)}, bf16[1,512,896]{2,1,0:T(8,128)(2,1)}, u32[]{:S(2)}) copy-start(bf16[1,512,896]{2,1,0:T(8,128)(2,1)} %param.7) | copy-start | bytes 2752516
  1.6 2.1 %copy-start.1 = (bf16[4,16,896]{2,1,0:T(8,128)(2,1)S(1)}, bf16[4,16,896]{2,1,0:T(8,128)(2,1)}, u32[]{:S(2)}) copy-start(bf16[4,16,896]{2,1,0:T(8,128)(2,1)} %tok_ref.1) | copy-start | bytes 344068
